TPU v7x, 512 devices: a whole 4x4x16 slice. The times are simulated.
512 devices in a mesh: ctx: 128 (over y, z, core), head: 4 (over x).
Axes of the slice: x: 4, y: 4, z: 16, core: 2. Of those that a mesh axis runs over, the one named last changes fastest.
Arguments:
- branch_q: bfloat16 [16384, 4, 1024], P('ctx', 'head'), may hold values from -6 to 6
- branch_k: bfloat16 [16384, 4, 128], P('ctx', 'head'), may hold values from -6 to 6
- branch_v: bfloat16 [16384, 4, 128], P('ctx', 'head'), may hold values from -6 to 6
- branch_o: bfloat16 [16384, 4, 1024], P('ctx', 'head'), may hold values from -4 to 4
- branch_dout: bfloat16 [16384, 4, 1024], P('ctx', 'head'), may hold values from -512 to 512
- prompt_q: bfloat16 [256, 4, 1024], P('ctx', 'head'), may hold values from -6 to 6
- prompt_k: bfloat16 [256, 4, 128], P('ctx', 'head'), may hold values from -6 to 6
- prompt_v: bfloat16 [256, 4, 128], P('ctx', 'head'), may hold values from -6 to 6
- prompt_o: bfloat16 [256, 4, 1024], P('ctx', 'head'), may hold values from -4 to 4
- prompt_dout: bfloat16 [256, 4, 1024], P('ctx', 'head'), may hold values from -512 to 512
- gains: float32 [2, 128], replicated, may hold values from 0.8 to 2
- parents: int32 [128], P('ctx'), may hold values from 0 to 128, as said below
- depth: int32 [16384], P('ctx'), may hold values from 128 to 1279, as said below
Outputs:
- branch_dq: bfloat16 [16384, 4, 1024], P('ctx', 'head')
- branch_dk: bfloat16 [16384, 4, 128], P('ctx', 'head')
- branch_dv: bfloat16 [16384, 4, 128], P('ctx', 'head')
- prompt_dq: bfloat16 [256, 4, 1024], P('ctx', 'head')
- prompt_dk: bfloat16 [256, 4, 128], P('ctx', 'head')
- prompt_dv: bfloat16 [256, 4, 128], P('ctx', 'head')
- gain_grads: float32 [2, 128], replicated
Inputs may be any that keep to these rules, and one draw needn't show every extreme that they name: `parents`: the parent of a branch block is a prompt block or an earlier branch block of the same subtree. A subtree is a run of consecutive branch blocks whose first block's parent is a prompt block; a run has at most 8 blocks, and some run has exactly 8. depth of a branch token = 128 times the number of its block's proper ancestor blocks, prompt blocks up to the fork included, plus its offset in its block.
All inputs are finite; a program needn't handle non-finite values.
Results may differ from a plain program's by a relative error of at most 0.0093.
Values may be sent and summed in bfloat16 or wider, within the bound.
A program may use at most 64 MiB of HBM per device.

v0:
```python
import jax
import jax.numpy as jnp
from jax import lax
from jax.sharding import PartitionSpec as P

BLK = 128
SUB = 8
PFX = 256
EPS = 1e-06
THETA = 1000000.0


def shifted(value, axis, steps):
    count = lax.axis_size(axis)
    leading, last = (max(0, -steps), min(count, count - steps))
    return lax.ppermute(value, axis, [(source, source + steps) for source in range(leading, last)])


def angles(positions, head_size):
    half_size = head_size // 2
    frequencies = THETA ** (-(jnp.arange(half_size, dtype=jnp.float32) * 2.0) / head_size)
    return positions.astype(jnp.float32)[:, None] * frequencies[None, :]


def rotate(values, angle_table):
    half_size = values.shape[-1] // 2
    cosine = jnp.cos(angle_table)
    sine_part = jnp.sin(angle_table)
    first_half = values[..., :half_size]
    second_half = values[..., half_size:]
    return jnp.concatenate(
        [
            first_half * cosine - second_half * sine_part,
            second_half * cosine + first_half * sine_part,
        ],
        axis=-1,
    )


def prepare(raw_values, gain_vector, angle_table):
    widened = raw_values.astype(jnp.float32)
    inverse = lax.rsqrt(jnp.mean(widened * widened, axis=-1, keepdims=True) + EPS)
    unit_values = widened * inverse
    rotated = rotate(unit_values * gain_vector, angle_table).astype(jnp.bfloat16)
    return (unit_values, inverse, rotated)


def norm_back(grad_rotated, unit_values, inverse, gain_vector, angle_table):
    grad_normed = rotate(grad_rotated, -angle_table)
    scaled = grad_normed * gain_vector
    grad_raw = (
        scaled - unit_values * jnp.mean(scaled * unit_values, axis=-1, keepdims=True)
    ) * inverse
    gain_part = jnp.sum((grad_normed * unit_values).reshape(-1, unit_values.shape[-1]), axis=0)
    return (grad_raw, gain_part)


def per_device(
    branch_q,
    branch_k,
    branch_v,
    branch_o,
    branch_dout,
    prompt_q,
    prompt_k,
    prompt_v,
    prompt_o,
    prompt_dout,
    gains,
    parents,
    depth,
):
    head_size = branch_k.shape[-1]
    tok_local = branch_k.shape[0]
    prompt_local = prompt_k.shape[0]
    group_size = branch_q.shape[-1] // head_size
    blocks_local = tok_local // BLK
    reach_back = (SUB + blocks_local - 2) // blocks_local
    prompt_blocks = PFX // BLK
    piece_size = 2 * BLK
    score_scale = head_size ** (-0.5)
    device = lax.axis_index("ctx")
    gain_q = gains[0]
    gain_k = gains[1]
    row_count = tok_local + prompt_local
    angle_branch = angles(depth, head_size)
    angle_prompt = angles(
        device * prompt_local + jnp.arange(prompt_local, dtype=jnp.int32), head_size
    )
    angle_rows = jnp.concatenate([angle_branch, angle_prompt])[:, None, :]
    queries = jnp.concatenate([branch_q[:, 0], prompt_q[:, 0]]).reshape(
        row_count, group_size, head_size
    )
    unit_q, inverse_q, rotated_q = prepare(queries, gain_q, angle_rows)
    unit_bk, inverse_bk, rotated_bk = prepare(branch_k[:, 0], gain_k, angle_branch)
    unit_pk, inverse_pk, rotated_pk = prepare(prompt_k[:, 0], gain_k, angle_prompt)
    value_local = branch_v[:, 0]
    prompt_keys, prompt_values = (
        lax.all_gather(rotated_pk, "ctx", axis=0, tiled=True),
        lax.all_gather(prompt_v[:, 0], "ctx", axis=0, tiled=True),
    )
    fetched = [(rotated_bk, value_local, parents)]
    for distance in range(1, reach_back + 1):
        fetched.insert(0, shifted((rotated_bk, value_local, parents), "ctx", distance))
    window_k = jnp.stack([member[0] for member in fetched])
    window_v = jnp.stack([member[1] for member in fetched])
    window_parents = jnp.stack([member[2] for member in fetched])
    window_blocks = (reach_back + 1) * blocks_local
    flat_parents = window_parents.reshape(window_blocks)
    first_block = (device - reach_back) * blocks_local
    slot_ids = jnp.arange(window_blocks, dtype=jnp.int32)

    def climb(step_index, climb_state):
        current, ancestors, fork_blocks = climb_state
        branchy = current >= prompt_blocks
        located = current - prompt_blocks - first_block
        matched = (slot_ids[None, :] == located[:, None]) & branchy[:, None]
        upward = jnp.sum(jnp.where(matched, flat_parents[None, :], 0), axis=1).astype(jnp.int32)
        return (
            jnp.where(branchy, upward, current),
            ancestors | matched,
            jnp.where(branchy, fork_blocks, current),
        )

    start_state = (
        device * blocks_local + jnp.arange(blocks_local, dtype=jnp.int32) + prompt_blocks,
        jnp.zeros((blocks_local, window_blocks), dtype=bool),
        jnp.zeros((blocks_local,), jnp.int32),
    )
    unused, ancestors, fork_blocks = lax.fori_loop(0, SUB + 1, climb, start_state)
    offsets = jnp.arange(BLK, dtype=jnp.int32)
    branch_limit = jnp.broadcast_to(
        (BLK * (fork_blocks + 1))[:, None], (blocks_local, BLK)
    ).reshape(tok_local)
    prompt_limit = device * prompt_local + jnp.arange(prompt_local, dtype=jnp.int32) + 1
    row_limit = jnp.concatenate([branch_limit, prompt_limit])
    branch_seen = jnp.broadcast_to(
        ancestors[:, None, :], (blocks_local, BLK, window_blocks)
    ).reshape(tok_local, window_blocks)
    row_seen = jnp.concatenate([branch_seen, jnp.zeros((prompt_local, window_blocks), dtype=bool)])
    branch_own = jnp.broadcast_to(
        (reach_back * blocks_local + jnp.arange(blocks_local, dtype=jnp.int32))[:, None],
        (blocks_local, BLK),
    ).reshape(tok_local)
    row_own = jnp.concatenate([branch_own, jnp.full((prompt_local,), -1, jnp.int32)])
    row_offset = jnp.concatenate(
        [jnp.tile(offsets, blocks_local), jnp.zeros((prompt_local,), jnp.int32)]
    )

    def piece_mask(key_start):
        key_ids = key_start + jnp.arange(piece_size, dtype=jnp.int32)
        prompt_key = key_ids < PFX
        window_pos = key_ids - PFX
        key_block = window_pos // BLK
        key_offset = window_pos % BLK
        prompt_ok = prompt_key[None, :] & (key_ids[None, :] < row_limit[:, None])
        block_seen = jnp.any(
            row_seen[:, :, None] & (key_block[None, None, :] == slot_ids[None, :, None]), axis=1
        )
        causal = (key_block[None, :] != row_own[:, None]) | (
            key_offset[None, :] <= row_offset[:, None]
        )
        return prompt_ok | jnp.logical_not(prompt_key)[None, :] & block_seen & causal

    key_total = PFX + window_blocks * BLK
    piece_count = key_total // piece_size
    all_keys = jnp.concatenate([prompt_keys, window_k.reshape(-1, head_size)]).reshape(
        piece_count, piece_size, head_size
    )
    all_values = jnp.concatenate([prompt_values, window_v.reshape(-1, head_size)]).reshape(
        piece_count, piece_size, head_size
    )
    key_starts = jnp.arange(piece_count, dtype=jnp.int32) * piece_size
    query_rows = rotated_q.reshape(row_count * group_size, head_size)
    grad_rows = jnp.concatenate([branch_dout[:, 0], prompt_dout[:, 0]]).reshape(
        row_count * group_size, head_size
    )
    out_rows = jnp.concatenate([branch_o[:, 0], prompt_o[:, 0]]).reshape(
        row_count * group_size, head_size
    )
    row_delta = jnp.sum(
        grad_rows.astype(jnp.float32) * out_rows.astype(jnp.float32), axis=-1
    ).reshape(row_count, group_size)

    def scores_of(key_piece):
        products = jnp.einsum(
            "qd,kd->qk", query_rows, key_piece, preferred_element_type=jnp.float32
        )
        return products.reshape(row_count, group_size, piece_size) * score_scale

    def add_total(running, scan_item):
        key_start, key_piece = scan_item
        visible = piece_mask(key_start)[:, None, :]
        return (
            running + jnp.sum(jnp.where(visible, jnp.exp(scores_of(key_piece)), 0.0), axis=-1),
            None,
        )

    totals, unused_rows = lax.scan(
        add_total, jnp.zeros((row_count, group_size), jnp.float32), (key_starts, all_keys)
    )
    log_total = jnp.log(totals)

    def back_piece(grad_q, scan_item):
        key_start, key_piece, value_piece = scan_item
        visible = piece_mask(key_start)[:, None, :]
        weights = jnp.where(visible, jnp.exp(scores_of(key_piece) - log_total[:, :, None]), 0.0)
        weight_half = weights.astype(jnp.bfloat16).reshape(row_count * group_size, piece_size)
        grad_v = jnp.einsum("qk,qd->kd", weight_half, grad_rows, preferred_element_type=jnp.float32)
        grad_p = jnp.einsum(
            "qd,kd->qk", grad_rows, value_piece, preferred_element_type=jnp.float32
        ).reshape(row_count, group_size, piece_size)
        grad_s = (
            (weights * (grad_p - row_delta[:, :, None]))
            .astype(jnp.bfloat16)
            .reshape(row_count * group_size, piece_size)
        )
        grad_k = (
            jnp.einsum("qk,qd->kd", grad_s, query_rows, preferred_element_type=jnp.float32)
            * score_scale
        )
        added = grad_q + jnp.einsum(
            "qk,kd->qd", grad_s, key_piece, preferred_element_type=jnp.float32
        )
        return (added, (grad_k, grad_v))

    grad_q, piece_grads = lax.scan(
        back_piece,
        jnp.zeros((row_count * group_size, head_size), jnp.float32),
        (key_starts, all_keys, all_values),
    )
    grad_keys = piece_grads[0].reshape(key_total, head_size)
    grad_values = piece_grads[1].reshape(key_total, head_size)
    prompt_gk, prompt_gv = (
        lax.psum_scatter(grad_keys[:PFX], "ctx", scatter_dimension=0, tiled=True),
        lax.psum_scatter(grad_values[:PFX], "ctx", scatter_dimension=0, tiled=True),
    )
    window_gk = grad_keys[PFX:].reshape(reach_back + 1, tok_local, head_size)
    window_gv = grad_values[PFX:].reshape(reach_back + 1, tok_local, head_size)
    total_k = window_gk[reach_back]
    total_v = window_gv[reach_back]
    for distance in range(1, reach_back + 1):
        back_k, back_v = (
            shifted(window_gk[reach_back - distance].astype(jnp.bfloat16), "ctx", -distance).astype(
                jnp.float32
            ),
            shifted(window_gv[reach_back - distance].astype(jnp.bfloat16), "ctx", -distance).astype(
                jnp.float32
            ),
        )
        total_k = total_k + back_k
        total_v = total_v + back_v
    grad_all_q = (grad_q * score_scale).reshape(row_count, group_size, head_size)
    raw_q, gain_part_q = norm_back(grad_all_q, unit_q, inverse_q, gain_q, angle_rows)
    raw_bk, gain_bk = norm_back(total_k, unit_bk, inverse_bk, gain_k, angle_branch)
    raw_pk, gain_pk = norm_back(prompt_gk, unit_pk, inverse_pk, gain_k, angle_prompt)
    sum_q, sum_k = lax.psum((gain_part_q, gain_bk + gain_pk), ("ctx", "head"))
    token_total = (tok_local + prompt_local) * lax.axis_size("ctx")
    head_total = lax.axis_size("head")
    factor_q = (token_total * head_total * group_size) ** (-0.5)
    factor_k = (token_total * head_total) ** (-0.5)
    gain_grads = jnp.stack([sum_q * factor_q, sum_k * factor_k])
    branch_dq = raw_q[:tok_local].reshape(tok_local, 1, group_size * head_size).astype(jnp.bfloat16)
    prompt_dq = (
        raw_q[tok_local:].reshape(prompt_local, 1, group_size * head_size).astype(jnp.bfloat16)
    )
    return (
        branch_dq,
        raw_bk[:, None].astype(jnp.bfloat16),
        total_v[:, None].astype(jnp.bfloat16),
        prompt_dq,
        raw_pk[:, None].astype(jnp.bfloat16),
        prompt_gv[:, None].astype(jnp.bfloat16),
        gain_grads,
    )


def solution(mesh):
    return jax.shard_map(
        per_device,
        mesh=mesh,
        in_specs=(
            P("ctx", "head", None),
            P("ctx", "head", None),
            P("ctx", "head", None),
            P("ctx", "head", None),
            P("ctx", "head", None),
            P("ctx", "head", None),
            P("ctx", "head", None),
            P("ctx", "head", None),
            P("ctx", "head", None),
            P("ctx", "head", None),
            P(),
            P("ctx"),
            P("ctx"),
        ),
        out_specs=(
            P("ctx", "head", None),
            P("ctx", "head", None),
            P("ctx", "head", None),
            P("ctx", "head", None),
            P("ctx", "head", None),
            P("ctx", "head", None),
            P(),
        ),
        check_vma=False,
    )
```

profile of v0, /device:TPU:1, one launch (start us, length us, event | category | flops | bytes accessed | tf_op | source)
XLA Modules:
  0.0 1014.4 jit_solution(6834789810668962888)
XLA Ops:
  10.8 10.2 %collective-permute-start.7 = (bf16[128,128]{1,0:T(8,128)(2,1)S(1)}, bf16[128,128]{1,0:T(8,128)(2,1)S(1)}, u32[]{:S(2)}, u32[]{:S(2)}) collective-permute-start(bf16[128,128]{1,0:T(8,128)(2,1)S(1)} %pad_maximum_fusion.8), channel_id=1, source_target_pairs={{0,28},{4,32},{8,36},{12,40},{16,44},{20,48},{24,52},{28,56},{32,6... | collective-permute-start | bytes 98312 | tf_op jit(solution)/shard_map/ppermute | solution.py:16
  21.0 6.3 collective-permute-start.8
  27.3 5.2 collective-permute-start.9
  32.5 3.1 collective-permute-start.10
  35.6 5.1 collective-permute-start
  43.2 72.9 %all-gather.1 = bf16[128,2,128]{2,1,0:T(2,128)(2,1)S(1)} all-gather(bf16[1,2,128]{2,1,0:T(2,128)(2,1)S(1)} %maximum_bitcast_fusion), channel_id=1, replica_groups=mesh['ctx'=128,'head'=4] {'ctx'}, dimensions={0}, use_global_device_ids=true | all-gather | bytes 66048 | tf_op jit(solution)/shard_map/all_gather | solution.py:99
  117.5 81.3 %all-gather = bf16[256,1,128]{2,1,0:T(2,128)(2,1)S(1)} all-gather(bf16[2,1,128]{2,1,0:T(2,128)(2,1)S(1)} %copy.30), channel_id=2, replica_groups=mesh['ctx'=128,'head'=4] {'ctx'}, dimensions={0}, use_global_device_ids=true | all-gather | bytes 66048 | tf_op jit(solution)/shard_map/all_gather | solution.py:100
  201.2 1.3 dynamic-slice
  203.2 3.9 collective-permute-start.1
  207.4 7.1 collective-permute-start.2
  214.8 4.9 collective-permute-start.3
  220.1 8.2 collective-permute-start.4
  228.6 3.1 collective-permute-start.5
  231.9 5.7 collective-permute-start.6
  238.5 5.8 collective-permute-start.11
  244.3 4.6 stack.93
  248.8 12.0 %while.48 = (s32[]{:T(128)}, s32[1]{0:T(128)}, pred[1,8]{1,0:T(4,128)(4,1)S(1)}, s32[1]{0:T(128)}, s32[]{:T(128)}, /*index=5*/s32[8,1]{0,1:T(1,128)S(1)}, s32[]{:T(128)}, s32[1]{0:T(128)}, s32[1]{0:T(128)}, s32[]{:T(128)}) while((s32[]{:T(128)}, s32[1]{0:T(128)}, pred[1,8]{1,0:T(4,128)(4,1)S(1)}, s32[1]{0:T(128)}, s32[]{:T(128)}, ...), condition=%wide.region_4.0_spmd.clone, body=%wide.region_2.4_spmd.clone.sunk | while | flops 71 | bytes 240 | solution.py:130
  260.9 5.7 collective-permute-start.12
  266.6 3.7 collective-permute-start.13
  270.3 4.0 collective-permute-start.14
  274.3 5.8 collective-permute-start.15
  280.1 5.7 collective-permute-start.16
  285.8 1.9 collective-permute-start.17
  287.8 9.6 collective-permute-start.18
  297.5 18.9 %while.49 = (s32[]{:T(128)}, f32[130,8]{1,0:T(8,128)S(1)}, s32[5]{0:T(128)S(1)}, s32[130]{0:T(256)S(1)}, pred[130,8]{1,0:T(8,128)(4,1)S(1)}, /*index=5*/bf16[5,2...) while((s32[]{:T(128)}, f32[130,8]{1,0:T(8,128)S(1)}, ...), condition=%wide.region_9.10_spmd.clone, body=%wide.region_6.0_spmd.clone.sunk | while | flops 69731088 | bytes 506427 | solution.py:199
  316.4 2.0 collective-permute-start.19
  318.4 2.9 collective-permute-start.20
  323.1 35.6 %while.50 = (s32[]{:T(128)}, f32[1040,128]{1,0:T(8,128)S(1)}, f32[5,256,128]{2,1,0:T(8,128)}, f32[5,256,128]{2,1,0:T(8,128)}, s32[5]{0:T(128)S(1)}, /*index=5*/s...) while((s32[]{:T(128)}, f32[1040,128]{1,0:T(8,128)S(1)}, ...), condition=%wide.wide.region_13.14_spmd.clone, body=%wide.wide.region_11.13_spmd.clone.sunk | while | flops 343723776 | bytes 7544631 | solution.py:227
  358.7 1.6 slice_bitcast_fusion.1
  363.4 1.9 collective-permute-start.21
  365.4 1.3 collective-permute-start.22
  366.7 1.3 collective-permute-start.23
  368.0 1.3 collective-permute-start.24
  369.3 1.3 collective-permute-start.25
  372.8 485.7 %all-reduce.9 = bf16[256,128]{1,0:T(8,128)(2,1)S(1)} all-reduce(f32[256,128]{1,0:T(8,128)S(1)} %slice_bitcast_fusion), channel_id=4, replica_groups=mesh['ctx'=128,'head'=4] {'ctx'}, use_global_device_ids=true, to_apply=%region_18.19.clone | all-reduce | flops 32768 | bytes 196608
  859.8 1.3 collective-permute-start.27
  863.1 7.5 collective-permute-start.28
  870.7 1.3 collective-permute-start.29
  872.0 1.3 collective-permute-start.30
  873.3 1.3 collective-permute-start.31
  874.6 1.3 collective-permute-start.32
  876.5 1.3 collective-permute-start.33
  877.8 1.3 collective-permute-start.34
  879.1 1.7 collective-permute-done.31
  880.8 4.1 collective-permute-done.32
  884.9 2.7 collective-permute-done.33
  887.6 5.2 collective-permute-done.34
  895.2 111.2 %all-reduce.4 = (f32[128]{0:T(128)S(1)}, f32[128]{0:T(128)S(1)}) all-reduce(f32[128]{0:T(128)S(1)} %add.378, f32[128]{0:T(128)S(1)} %get-tuple-element.496), channel_id=1, replica_groups=mesh['ctx'=128,'head'=4] {'ctx','head'}, use_global_device_ids=true, to_apply=%region_23.24 | all-reduce | flops 256 | bytes 2048 | tf_op jit(solution)/shard_map/psum | solution.py:257
  (279 shorter events, 85.5 us)
Async XLA Ops:
  7.2 110.0 %copy-start.11 = (bf16[2,1,1024]{2,0,1:T(2,128)(2,1)S(1)}, bf16[2,1,1024]{2,0,1:T(2,128)(2,1)}, u32[]{:S(2)}) copy-start(bf16[2,1,1024]{2,0,1:T(2,128)(2,1)} %param.24) | copy-start | bytes 12292
  7.2 110.3 %copy-start.12 = (bf16[2,1,128]{2,0,1:T(2,128)(2,1)S(1)}, bf16[2,1,128]{2,0,1:T(2,128)(2,1)}, u32[]{:S(2)}) copy-start(bf16[2,1,128]{2,0,1:T(2,128)(2,1)} %param.26) | copy-start | bytes 1540
  7.2 191.6 %copy-start.4 = (bf16[128,1,1024]{2,0,1:T(8,128)(2,1)S(1)}, bf16[128,1,1024]{2,0,1:T(8,128)(2,1)}, u32[]{:S(2)}) copy-start(bf16[128,1,1024]{2,0,1:T(8,128)(2,1)} %param.23) | copy-start | bytes 786436
  7.2 191.6 %copy-start.9 = (bf16[2,1,1024]{2,0,1:T(2,128)(2,1)S(1)}, bf16[2,1,1024]{2,0,1:T(2,128)(2,1)}, u32[]{:S(2)}) copy-start(bf16[2,1,1024]{2,0,1:T(2,128)(2,1)} %param.28) | copy-start | bytes 12292
  7.2 887.0 %all-reduce.8.cloned.1.call-start = ((), (), s32[]{:S(2)}) async-start(), calls=%async_computation | async-start | bytes 262144
  10.8 250.1 %collective-permute-start.7 = (bf16[128,128]{1,0:T(8,128)(2,1)S(1)}, bf16[128,128]{1,0:T(8,128)(2,1)S(1)}, u32[]{:S(2)}, u32[]{:S(2)}) collective-permute-start(bf16[128,128]{1,0:T(8,128)(2,1)S(1)} %pad_maximum_fusion.8), channel_id=1, source_target_pairs={{0,28},{4,32},{8,36},{12,40},{16,44},{20,48},{24,52},{28,56},{32,6... | collective-permute-start | bytes 98312 | tf_op jit(solution)/shard_map/ppermute | solution.py:16
  21.0 245.6 %collective-permute-start.8 = (bf16[128,128]{1,0:T(8,128)(2,1)S(1)}, bf16[128,128]{1,0:T(8,128)(2,1)S(1)}, u32[]{:S(2)}, u32[]{:S(2)}) collective-permute-start(bf16[128,128]{1,0:T(8,128)(2,1)S(1)} %pad_maximum_fusion.8), channel_id=1, source_target_pairs={{0,24},{4,28},{8,32},{12,36},{16,40},{20,44},{24,48},{28,52},{32,5... | collective-permute-start | bytes 98312 | tf_op jit(solution)/shard_map/ppermute | solution.py:16
  27.3 243.0 %collective-permute-start.9 = (bf16[128,128]{1,0:T(8,128)(2,1)S(1)}, bf16[128,128]{1,0:T(8,128)(2,1)S(1)}, u32[]{:S(2)}, u32[]{:S(2)}) collective-permute-start(bf16[128,128]{1,0:T(8,128)(2,1)S(1)} %pad_maximum_fusion.8), channel_id=1, source_target_pairs={{0,20},{4,24},{8,28},{12,32},{16,36},{20,40},{24,44},{28,48},{32,5... | collective-permute-start | bytes 98312 | tf_op jit(solution)/shard_map/ppermute | solution.py:16
  32.5 241.8 %collective-permute-start.10 = (bf16[128,128]{1,0:T(8,128)(2,1)S(1)}, bf16[128,128]{1,0:T(8,128)(2,1)S(1)}, u32[]{:S(2)}, u32[]{:S(2)}) collective-permute-start(bf16[128,128]{1,0:T(8,128)(2,1)S(1)} %pad_maximum_fusion.8), channel_id=1, source_target_pairs={{0,16},{4,20},{8,24},{12,28},{16,32},{20,36},{24,40},{28,44},{32,4... | collective-permute-start | bytes 98312 | tf_op jit(solution)/shard_map/ppermute | solution.py:16
  35.6 167.6 %collective-permute-start = (s32[1]{0:T(128)}, s32[1]{0:T(128)}, u32[]{:S(2)}, u32[]{:S(2)}) collective-permute-start(s32[1]{0:T(128)} %param.30), channel_id=1, source_target_pairs={{0,28},{4,32},{8,36},{12,40},{16,44},{20,48},{24,52},{28,56},{32,6... | collective-permute-start | bytes 20 | tf_op jit(solution)/shard_map/ppermute | solution.py:16
  117.2 81.8 %copy-start.3 = (bf16[128,1,1024]{2,0,1:T(8,128)(2,1)S(1)}, bf16[128,1,1024]{2,0,1:T(8,128)(2,1)}, u32[]{:S(2)}) copy-start(bf16[128,1,1024]{2,0,1:T(8,128)(2,1)} %param.22) | copy-start | bytes 786436
  117.2 81.8 %copy-start.10 = (bf16[2,1,1024]{2,0,1:T(2,128)(2,1)S(1)}, bf16[2,1,1024]{2,0,1:T(2,128)(2,1)}, u32[]{:S(2)}) copy-start(bf16[2,1,1024]{2,0,1:T(2,128)(2,1)} %param.27) | copy-start | bytes 12292
  200.7 69.6 %copy-start.7 = (bf16[128,1,128]{2,0,1:T(8,128)(2,1)S(1)}, bf16[128,1,128]{2,0,1:T(8,128)(2,1)}, u32[]{:S(2)}) copy-start(bf16[128,1,128]{2,0,1:T(8,128)(2,1)} %param.21) | copy-start | bytes 98308
  200.9 96.6 %copy-start.5 = (s32[130]{0:T(256)S(1)}, s32[130]{0:T(256)}, u32[]{:S(2)}) copy-start(s32[130]{0:T(256)} %constant.212.clone.2) | copy-start | bytes 1564
  200.9 96.6 %copy-start.6 = (s32[130]{0:T(256)S(1)}, s32[130]{0:T(256)}, u32[]{:S(2)}) copy-start(s32[130]{0:T(256)} %constant.214.clone.2) | copy-start | bytes 1564
  203.2 4.2 collective-permute-start.1
  207.4 7.4 collective-permute-start.2
  214.8 5.3 collective-permute-start.3
  220.1 8.5 collective-permute-start.4
  228.6 3.4 collective-permute-start.5
  231.9 6.5 collective-permute-start.6
  238.5 41.7 %collective-permute-start.11 = (bf16[128,128]{1,0:T(8,128)(2,1)S(1)}, bf16[128,128]{1,0:T(8,128)(2,1)S(1)}, u32[]{:S(2)}, u32[]{:S(2)}) collective-permute-start(bf16[128,128]{1,0:T(8,128)(2,1)S(1)} %pad_maximum_fusion.8), channel_id=1, source_target_pairs={{0,12},{4,16},{8,20},{12,24},{16,28},{20,32},{24,36},{28,40},{32,4... | collective-permute-start | bytes 98312 | tf_op jit(solution)/shard_map/ppermute | solution.py:16
  260.9 24.9 %collective-permute-start.12 = (bf16[128,128]{1,0:T(8,128)(2,1)S(1)}, bf16[128,128]{1,0:T(8,128)(2,1)S(1)}, u32[]{:S(2)}, u32[]{:S(2)}) collective-permute-start(bf16[128,128]{1,0:T(8,128)(2,1)S(1)} %pad_maximum_fusion.8), channel_id=1, source_target_pairs={{0,8},{4,12},{8,16},{12,20},{16,24},{20,28},{24,32},{28,36},{32,40... | collective-permute-start | bytes 98312 | tf_op jit(solution)/shard_map/ppermute | solution.py:16
  266.6 21.2 %collective-permute-start.13 = (bf16[128,128]{1,0:T(8,128)(2,1)S(1)}, bf16[128,128]{1,0:T(8,128)(2,1)S(1)}, u32[]{:S(2)}, u32[]{:S(2)}) collective-permute-start(bf16[128,128]{1,0:T(8,128)(2,1)S(1)} %pad_maximum_fusion.8), channel_id=1, source_target_pairs={{0,4},{4,8},{8,12},{12,16},{16,20},{20,24},{24,28},{28,32},{32,36}... | collective-permute-start | bytes 98312 | tf_op jit(solution)/shard_map/ppermute | solution.py:16
  270.3 46.1 %collective-permute-start.14 = (bf16[128,128]{1,0:T(8,128)(2,1)S(1)}, bf16[128,128]{1,0:T(8,128)(2,1)S(1)}, u32[]{:S(2)}, u32[]{:S(2)}) collective-permute-start(bf16[128,128]{1,0:T(8,128)(2,1)S(1)} %bitcast.351), channel_id=1, source_target_pairs={{0,28},{4,32},{8,36},{12,40},{16,44},{20,48},{24,52},{28,56},{32,6... | collective-permute-start | bytes 98312 | tf_op jit(solution)/shard_map/ppermute | solution.py:16
  274.3 44.1 %collective-permute-start.15 = (bf16[128,128]{1,0:T(8,128)(2,1)S(1)}, bf16[128,128]{1,0:T(8,128)(2,1)S(1)}, u32[]{:S(2)}, u32[]{:S(2)}) collective-permute-start(bf16[128,128]{1,0:T(8,128)(2,1)S(1)} %bitcast.352), channel_id=1, source_target_pairs={{0,24},{4,28},{8,32},{12,36},{16,40},{20,44},{24,48},{28,52},{32,5... | collective-permute-start | bytes 98312 | tf_op jit(solution)/shard_map/ppermute | solution.py:16
  280.1 41.2 %collective-permute-start.16 = (bf16[128,128]{1,0:T(8,128)(2,1)S(1)}, bf16[128,128]{1,0:T(8,128)(2,1)S(1)}, u32[]{:S(2)}, u32[]{:S(2)}) collective-permute-start(bf16[128,128]{1,0:T(8,128)(2,1)S(1)} %bitcast.353), channel_id=1, source_target_pairs={{0,20},{4,24},{8,28},{12,32},{16,36},{20,40},{24,44},{28,48},{32,5... | collective-permute-start | bytes 98312 | tf_op jit(solution)/shard_map/ppermute | solution.py:16
  285.8 35.5 %collective-permute-start.17 = (bf16[128,128]{1,0:T(8,128)(2,1)S(1)}, bf16[128,128]{1,0:T(8,128)(2,1)S(1)}, u32[]{:S(2)}, u32[]{:S(2)}) collective-permute-start(bf16[128,128]{1,0:T(8,128)(2,1)S(1)} %bitcast.354), channel_id=1, source_target_pairs={{0,16},{4,20},{8,24},{12,28},{16,32},{20,36},{24,40},{28,44},{32,4... | collective-permute-start | bytes 98312 | tf_op jit(solution)/shard_map/ppermute | solution.py:16
  287.8 33.6 %collective-permute-start.18 = (bf16[128,128]{1,0:T(8,128)(2,1)S(1)}, bf16[128,128]{1,0:T(8,128)(2,1)S(1)}, u32[]{:S(2)}, u32[]{:S(2)}) collective-permute-start(bf16[128,128]{1,0:T(8,128)(2,1)S(1)} %bitcast.355), channel_id=1, source_target_pairs={{0,12},{4,16},{8,20},{12,24},{16,28},{20,32},{24,36},{28,40},{32,4... | collective-permute-start | bytes 98312 | tf_op jit(solution)/shard_map/ppermute | solution.py:16
  316.4 5.0 collective-permute-start.19
  318.4 3.9 collective-permute-start.20
  321.5 1.6 copy-start.2
  363.4 495.1 %collective-permute-start.21 = (bf16[128,128]{1,0:T(8,128)(2,1)S(1)}, bf16[128,128]{1,0:T(8,128)(2,1)S(1)}, u32[]{:S(2)}, u32[]{:S(2)}) collective-permute-start(bf16[128,128]{1,0:T(8,128)(2,1)S(1)} %get-tuple-element.575), channel_id=1, source_target_pairs={{4,0},{8,4},{12,8},{16,12},{20,16},{24,20},{28,24},{32,28},{36,32}... | collective-permute-start | bytes 98312 | tf_op jit(solution)/shard_map/ppermute | solution.py:16
  365.4 494.4 %collective-permute-start.22 = (bf16[128,128]{1,0:T(8,128)(2,1)S(1)}, bf16[128,128]{1,0:T(8,128)(2,1)S(1)}, u32[]{:S(2)}, u32[]{:S(2)}) collective-permute-start(bf16[128,128]{1,0:T(8,128)(2,1)S(1)} %get-tuple-element.581), channel_id=1, source_target_pairs={{8,0},{12,4},{16,8},{20,12},{24,16},{28,20},{32,24},{36,28},{40,32... | collective-permute-start | bytes 98312 | tf_op jit(solution)/shard_map/ppermute | solution.py:16
  366.7 496.4 %collective-permute-start.23 = (bf16[128,128]{1,0:T(8,128)(2,1)S(1)}, bf16[128,128]{1,0:T(8,128)(2,1)S(1)}, u32[]{:S(2)}, u32[]{:S(2)}) collective-permute-start(bf16[128,128]{1,0:T(8,128)(2,1)S(1)} %get-tuple-element.580), channel_id=1, source_target_pairs={{12,0},{16,4},{20,8},{24,12},{28,16},{32,20},{36,24},{40,28},{44,3... | collective-permute-start | bytes 98312 | tf_op jit(solution)/shard_map/ppermute | solution.py:16
  368.0 502.7 %collective-permute-start.24 = (bf16[128,128]{1,0:T(8,128)(2,1)S(1)}, bf16[128,128]{1,0:T(8,128)(2,1)S(1)}, u32[]{:S(2)}, u32[]{:S(2)}) collective-permute-start(bf16[128,128]{1,0:T(8,128)(2,1)S(1)} %get-tuple-element.579), channel_id=1, source_target_pairs={{16,0},{20,4},{24,8},{28,12},{32,16},{36,20},{40,24},{44,28},{48,3... | collective-permute-start | bytes 98312 | tf_op jit(solution)/shard_map/ppermute | solution.py:16
  369.3 502.7 %collective-permute-start.25 = (bf16[128,128]{1,0:T(8,128)(2,1)S(1)}, bf16[128,128]{1,0:T(8,128)(2,1)S(1)}, u32[]{:S(2)}, u32[]{:S(2)}) collective-permute-start(bf16[128,128]{1,0:T(8,128)(2,1)S(1)} %get-tuple-element.578), channel_id=1, source_target_pairs={{20,0},{24,4},{28,8},{32,12},{36,16},{40,20},{44,24},{48,28},{52,3... | collective-permute-start | bytes 98312 | tf_op jit(solution)/shard_map/ppermute | solution.py:16
  372.8 503.5 %copy-start = (bf16[128,1,128]{2,0,1:T(8,128)(2,1)S(1)}, bf16[128,1,128]{2,0,1:T(8,128)(2,1)}, u32[]{:S(2)}) copy-start(bf16[128,1,128]{2,0,1:T(8,128)(2,1)} %param.20) | copy-start | bytes 98308
  858.5 14.8 %collective-permute-start.26 = (bf16[128,128]{1,0:T(8,128)(2,1)S(1)}, bf16[128,128]{1,0:T(8,128)(2,1)S(1)}, u32[]{:S(2)}, u32[]{:S(2)}) collective-permute-start(bf16[128,128]{1,0:T(8,128)(2,1)S(1)} %get-tuple-element.577), channel_id=1, source_target_pairs={{24,0},{28,4},{32,8},{36,12},{40,16},{44,20},{48,24},{52,28},{56,3... | collective-permute-start | bytes 98312 | tf_op jit(solution)/shard_map/ppermute | solution.py:16
  859.8 14.8 %collective-permute-start.27 = (bf16[128,128]{1,0:T(8,128)(2,1)S(1)}, bf16[128,128]{1,0:T(8,128)(2,1)S(1)}, u32[]{:S(2)}, u32[]{:S(2)}) collective-permute-start(bf16[128,128]{1,0:T(8,128)(2,1)S(1)} %get-tuple-element.576), channel_id=1, source_target_pairs={{28,0},{32,4},{36,8},{40,12},{44,16},{48,20},{52,24},{56,28},{60,3... | collective-permute-start | bytes 98312 | tf_op jit(solution)/shard_map/ppermute | solution.py:16
  861.7 33.3 %copy-start.8 = (bf16[2,1,128]{2,0,1:T(2,128)(2,1)S(1)}, bf16[2,1,128]{2,0,1:T(2,128)(2,1)}, u32[]{:S(2)}) copy-start(bf16[2,1,128]{2,0,1:T(2,128)(2,1)} %param.25) | copy-start | bytes 1540
  863.1 13.4 %collective-permute-start.28 = (bf16[128,128]{1,0:T(8,128)(2,1)S(1)}, bf16[128,128]{1,0:T(8,128)(2,1)S(1)}, u32[]{:S(2)}, u32[]{:S(2)}) collective-permute-start(bf16[128,128]{1,0:T(8,128)(2,1)S(1)} %get-tuple-element.568), channel_id=1, source_target_pairs={{4,0},{8,4},{12,8},{16,12},{20,16},{24,20},{28,24},{32,28},{36,32}... | collective-permute-start | bytes 98312 | tf_op jit(solution)/shard_map/ppermute | solution.py:16
  870.7 7.1 collective-permute-start.29
  872.0 7.1 collective-permute-start.30
  873.3 7.5 collective-permute-start.31
  874.6 10.3 %collective-permute-start.32 = (bf16[128,128]{1,0:T(8,128)(2,1)S(1)}, bf16[128,128]{1,0:T(8,128)(2,1)S(1)}, u32[]{:S(2)}, u32[]{:S(2)}) collective-permute-start(bf16[128,128]{1,0:T(8,128)(2,1)S(1)} %get-tuple-element.571), channel_id=1, source_target_pairs={{20,0},{24,4},{28,8},{32,12},{36,16},{40,20},{44,24},{48,28},{52,3... | collective-permute-start | bytes 98312 | tf_op jit(solution)/shard_map/ppermute | solution.py:16
  876.5 11.1 %collective-permute-start.33 = (bf16[128,128]{1,0:T(8,128)(2,1)S(1)}, bf16[128,128]{1,0:T(8,128)(2,1)S(1)}, u32[]{:S(2)}, u32[]{:S(2)}) collective-permute-start(bf16[128,128]{1,0:T(8,128)(2,1)S(1)} %get-tuple-element.570), channel_id=1, source_target_pairs={{24,0},{28,4},{32,8},{36,12},{40,16},{44,20},{48,24},{52,28},{56,3... | collective-permute-start | bytes 98312 | tf_op jit(solution)/shard_map/ppermute | solution.py:16
  877.8 15.0 %collective-permute-start.34 = (bf16[128,128]{1,0:T(8,128)(2,1)S(1)}, bf16[128,128]{1,0:T(8,128)(2,1)S(1)}, u32[]{:S(2)}, u32[]{:S(2)}) collective-permute-start(bf16[128,128]{1,0:T(8,128)(2,1)S(1)} %get-tuple-element.569), channel_id=1, source_target_pairs={{28,0},{32,4},{36,8},{40,12},{44,16},{48,20},{52,24},{56,28},{60,3... | collective-permute-start | bytes 98312 | tf_op jit(solution)/shard_map/ppermute | solution.py:16
  (1 other events, 0.9 us)
Sparse Core Ops, SparseCore 0:
  363.5 318.1 all-reduce.7
where the time goes:
time: 1020 us; the launch traced here: 1010 us
  blocking collectives  751 us (74%)
  starting transfers between devices  135 us (13%)
  other arithmetic  43.4 us (4%)
  local copies, waits for them, and re-layouts  22.6 us (2%)
  matrix products  22.5 us (2%)
  waiting for transfers between devices  16.9 us (2%)
  between operations  16.4 us (2%)
    unnamed x1, blocking collectives  486 us
    ppermute x35, starting transfers between devices, shifted(): lax.ppermute(value, axis, [(source, source + steps) for source in range(l...  135 us
    psum x1, blocking collectives, per_device(): sum_q, sum_k = lax.psum((gain_part_q, gain_bk + gain_pk), ('ctx', 'head'))  111 us
    all_gather x1, blocking collectives, per_device(): lax.all_gather(prompt_v[:, 0], 'ctx', axis=0, tiled=True)  81.3 us
    all_gather x1, blocking collectives, per_device(): lax.all_gather(rotated_pk, 'ctx', axis=0, tiled=True)  72.9 us
  transfers between devices with their start and end apart: 36, of which 11 were waited for; matrix products, arithmetic and copies ran while one was open for 4% of the time, Pallas kernels for 0%

commit v1 on v0

--- a/solution.py
+++ b/solution.py
@@ -97,7 +97,9 @@
     value_local = branch_v[:, 0]
     prompt_keys, prompt_values = (
         lax.all_gather(rotated_pk, "ctx", axis=0, tiled=True),
-        lax.all_gather(prompt_v[:, 0], "ctx", axis=0, tiled=True),
+        jnp.concatenate(
+            lax.all_to_all(jnp.stack([prompt_v[:, 0]] * lax.axis_size("ctx")), "ctx", 0, 0), axis=0
+        ),
     )
     fetched = [(rotated_bk, value_local, parents)]
     for distance in range(1, reach_back + 1):

time: 1020 us -> 955 us (0.936)
  blocking collectives: 751 us -> 675 us
  starting transfers between devices: 135 us -> 147 us
    all_gather x1 -> x0, blocking collectives: 81.3 us -> none  [per_device(): lax.all_gather(prompt_v[:, 0], 'ctx', axis=0, tiled=True)]
    all_to_all x0 -> x1, starting transfers between devices: none -> 11.6 us  [per_device(): lax.all_to_all(jnp.stack([prompt_v[:, 0]] * lax.axis_size('ctx')), 'ctx',...]
  transfers between devices with their start and end apart: 36 -> 37, of which waited for: 11 -> 11; matrix products, arithmetic and copies ran while one was open for 4% -> 4% of each run, Pallas kernels for 0% -> 0%
where the time goes in v1:
time: 955 us; the launch traced here: 952 us
  blocking collectives  675 us (71%)
  starting transfers between devices  147 us (15%)
  other arithmetic  43.4 us (5%)
  local copies, waits for them, and re-layouts  23.9 us (3%)
  matrix products  22.5 us (2%)
  waiting for transfers between devices  16.9 us (2%)
  between operations  16.4 us (2%)
    unnamed x1, blocking collectives  486 us
    ppermute x35, starting transfers between devices, shifted(): lax.ppermute(value, axis, [(source, source + steps) for source in range(l...  136 us
    psum x1, blocking collectives, per_device(): sum_q, sum_k = lax.psum((gain_part_q, gain_bk + gain_pk), ('ctx', 'head'))  111 us
    all_gather x1, blocking collectives, per_device(): lax.all_gather(rotated_pk, 'ctx', axis=0, tiled=True)  78.1 us
  transfers between devices with their start and end apart: 37, of which 11 were waited for; matrix products, arithmetic and copies ran while one was open for 4% of the time, Pallas kernels for 0%

profile of v1, /device:TPU:1, one launch (start us, length us, event | category | flops | bytes accessed | tf_op | source)
XLA Modules:
  0.0 952.4 jit_solution(14283316539559308929)
XLA Ops:
  10.8 10.2 %collective-permute-start.7 = (bf16[128,128]{1,0:T(8,128)(2,1)S(1)}, bf16[128,128]{1,0:T(8,128)(2,1)S(1)}, u32[]{:S(2)}, u32[]{:S(2)}) collective-permute-start(bf16[128,128]{1,0:T(8,128)(2,1)S(1)} %pad_maximum_fusion.8), channel_id=1, source_target_pairs={{0,28},{4,32},{8,36},{12,40},{16,44},{20,48},{24,52},{28,56},{32,6... | collective-permute-start | bytes 98312 | tf_op jit(solution)/shard_map/ppermute | solution.py:16
  21.0 6.3 collective-permute-start.8
  27.2 5.2 collective-permute-start.9
  32.5 3.1 collective-permute-start.10
  35.6 5.1 collective-permute-start
  40.7 1.3 stack.105
  42.0 11.6 %all-to-all-start = ((bf16[128,2,128]{2,1,0:T(2,128)(2,1)}), bf16[128,2,128]{2,1,0:T(2,128)(2,1)S(1)}, u32[]{:S(2)}, u32[]{:S(2)}) async-start(bf16[128,2,128]{2,1,0:T(2,128)(2,1)} %stack.105), calls=%async_computation | async-start | bytes 131072 | tf_op jit(solution)/shard_map/all_to_all | solution.py:101
  56.1 78.1 %all-gather = bf16[128,2,128]{2,1,0:T(2,128)(2,1)S(1)} all-gather(bf16[1,2,128]{2,1,0:T(2,128)(2,1)S(1)} %maximum_bitcast_fusion), channel_id=1, replica_groups=mesh['ctx'=128,'head'=4] {'ctx'}, dimensions={0}, use_global_device_ids=true | all-gather | bytes 66048 | tf_op jit(solution)/shard_map/all_gather | solution.py:99
  138.0 1.4 dynamic-slice
  140.1 3.4 collective-permute-start.1
  143.8 7.8 collective-permute-start.2
  151.9 5.6 collective-permute-start.3
  157.8 9.3 collective-permute-start.4
  167.3 2.2 collective-permute-start.5
  169.8 6.4 collective-permute-start.6
  177.1 5.8 collective-permute-start.11
  182.9 4.6 stack.96
  187.4 12.0 %while.48 = (s32[]{:T(128)}, s32[1]{0:T(128)}, pred[1,8]{1,0:T(4,128)(4,1)S(1)}, s32[1]{0:T(128)}, s32[]{:T(128)}, /*index=5*/s32[8,1]{0,1:T(1,128)S(1)}, s32[]{:T(128)}, s32[1]{0:T(128)}, s32[1]{0:T(128)}, s32[]{:T(128)}) while((s32[]{:T(128)}, s32[1]{0:T(128)}, pred[1,8]{1,0:T(4,128)(4,1)S(1)}, s32[1]{0:T(128)}, s32[]{:T(128)}, ...), condition=%wide.region_4.0_spmd.clone, body=%wide.region_2.4_spmd.clone.sunk | while | flops 71 | bytes 240 | solution.py:132
  199.5 5.7 collective-permute-start.12
  205.2 3.7 collective-permute-start.13
  208.9 4.0 collective-permute-start.14
  212.9 4.8 collective-permute-start.15
  217.8 3.7 collective-permute-start.16
  221.5 3.9 collective-permute-start.17
  225.5 9.6 %collective-permute-start.18 = (bf16[128,128]{1,0:T(8,128)(2,1)S(1)}, bf16[128,128]{1,0:T(8,128)(2,1)S(1)}, u32[]{:S(2)}, u32[]{:S(2)}) collective-permute-start(bf16[128,128]{1,0:T(8,128)(2,1)S(1)} %bitcast.354), channel_id=1, source_target_pairs={{0,12},{4,16},{8,20},{12,24},{16,28},{20,32},{24,36},{28,40},{32,4... | collective-permute-start | bytes 98312 | tf_op jit(solution)/shard_map/ppermute | solution.py:16
  235.2 18.9 %while.49 = (s32[]{:T(128)}, f32[130,8]{1,0:T(8,128)S(1)}, s32[5]{0:T(128)S(1)}, s32[130]{0:T(256)S(1)}, pred[130,8]{1,0:T(8,128)(4,1)S(1)}, /*index=5*/bf16[5,2...) while((s32[]{:T(128)}, f32[130,8]{1,0:T(8,128)S(1)}, ...), condition=%wide.region_9.10_spmd.clone, body=%wide.region_6.0_spmd.clone.sunk | while | flops 69731088 | bytes 506427 | solution.py:201
  254.1 1.9 collective-permute-start.19
  256.1 2.9 collective-permute-start.20
  260.9 35.5 %while.50 = (s32[]{:T(128)}, f32[1040,128]{1,0:T(8,128)S(1)}, f32[5,256,128]{2,1,0:T(8,128)}, f32[5,256,128]{2,1,0:T(8,128)}, s32[5]{0:T(128)S(1)}, /*index=5*/s...) while((s32[]{:T(128)}, f32[1040,128]{1,0:T(8,128)S(1)}, ...), condition=%wide.wide.region_13.14_spmd.clone, body=%wide.wide.region_11.13_spmd.clone.sunk | while | flops 343723776 | bytes 7544631 | solution.py:229
  296.4 1.6 slice_bitcast_fusion.1
  301.2 1.9 collective-permute-start.21
  303.1 1.3 collective-permute-start.22
  304.4 1.3 collective-permute-start.23
  305.7 1.3 collective-permute-start.24
  307.0 1.5 collective-permute-start.25
  310.7 485.7 %all-reduce.9 = bf16[256,128]{1,0:T(8,128)(2,1)S(1)} all-reduce(f32[256,128]{1,0:T(8,128)S(1)} %slice_bitcast_fusion), channel_id=3, replica_groups=mesh['ctx'=128,'head'=4] {'ctx'}, use_global_device_ids=true, to_apply=%region_18.19.clone | all-reduce | flops 32768 | bytes 196608
  797.7 1.3 collective-permute-start.27
  801.0 7.5 collective-permute-start.28
  808.6 1.3 collective-permute-start.29
  809.9 1.3 collective-permute-start.30
  811.2 1.3 collective-permute-start.31
  812.5 1.3 collective-permute-start.32
  814.4 1.3 collective-permute-start.33
  817.0 1.7 collective-permute-done.31
  818.7 4.1 collective-permute-done.32
  822.8 2.7 collective-permute-done.33
  825.5 5.2 collective-permute-done.34
  833.1 111.3 %all-reduce.4 = (f32[128]{0:T(128)S(1)}, f32[128]{0:T(128)S(1)}) all-reduce(f32[128]{0:T(128)S(1)} %add.378, f32[128]{0:T(128)S(1)} %get-tuple-element.496), channel_id=1, replica_groups=mesh['ctx'=128,'head'=4] {'ctx','head'}, use_global_device_ids=true, to_apply=%region_23.24 | all-reduce | flops 256 | bytes 2048 | tf_op jit(solution)/shard_map/psum | solution.py:259
  (277 shorter events, 86.9 us)
Async XLA Ops:
  7.2 128.1 %copy-start.11 = (bf16[2,1,1024]{2,0,1:T(2,128)(2,1)S(1)}, bf16[2,1,1024]{2,0,1:T(2,128)(2,1)}, u32[]{:S(2)}) copy-start(bf16[2,1,1024]{2,0,1:T(2,128)(2,1)} %param.24) | copy-start | bytes 12292
  7.2 128.4 %copy-start.4 = (bf16[128,1,1024]{2,0,1:T(8,128)(2,1)S(1)}, bf16[128,1,1024]{2,0,1:T(8,128)(2,1)}, u32[]{:S(2)}) copy-start(bf16[128,1,1024]{2,0,1:T(8,128)(2,1)} %param.23) | copy-start | bytes 786436
  7.2 128.4 %copy-start.9 = (bf16[2,1,1024]{2,0,1:T(2,128)(2,1)S(1)}, bf16[2,1,1024]{2,0,1:T(2,128)(2,1)}, u32[]{:S(2)}) copy-start(bf16[2,1,1024]{2,0,1:T(2,128)(2,1)} %param.28) | copy-start | bytes 12292
  10.8 188.7 %collective-permute-start.7 = (bf16[128,128]{1,0:T(8,128)(2,1)S(1)}, bf16[128,128]{1,0:T(8,128)(2,1)S(1)}, u32[]{:S(2)}, u32[]{:S(2)}) collective-permute-start(bf16[128,128]{1,0:T(8,128)(2,1)S(1)} %pad_maximum_fusion.8), channel_id=1, source_target_pairs={{0,28},{4,32},{8,36},{12,40},{16,44},{20,48},{24,52},{28,56},{32,6... | collective-permute-start | bytes 98312 | tf_op jit(solution)/shard_map/ppermute | solution.py:16
  21.0 184.2 %collective-permute-start.8 = (bf16[128,128]{1,0:T(8,128)(2,1)S(1)}, bf16[128,128]{1,0:T(8,128)(2,1)S(1)}, u32[]{:S(2)}, u32[]{:S(2)}) collective-permute-start(bf16[128,128]{1,0:T(8,128)(2,1)S(1)} %pad_maximum_fusion.8), channel_id=1, source_target_pairs={{0,24},{4,28},{8,32},{12,36},{16,40},{20,44},{24,48},{28,52},{32,5... | collective-permute-start | bytes 98312 | tf_op jit(solution)/shard_map/ppermute | solution.py:16
  27.2 181.7 %collective-permute-start.9 = (bf16[128,128]{1,0:T(8,128)(2,1)S(1)}, bf16[128,128]{1,0:T(8,128)(2,1)S(1)}, u32[]{:S(2)}, u32[]{:S(2)}) collective-permute-start(bf16[128,128]{1,0:T(8,128)(2,1)S(1)} %pad_maximum_fusion.8), channel_id=1, source_target_pairs={{0,20},{4,24},{8,28},{12,32},{16,36},{20,40},{24,44},{28,48},{32,5... | collective-permute-start | bytes 98312 | tf_op jit(solution)/shard_map/ppermute | solution.py:16
  32.5 180.5 %collective-permute-start.10 = (bf16[128,128]{1,0:T(8,128)(2,1)S(1)}, bf16[128,128]{1,0:T(8,128)(2,1)S(1)}, u32[]{:S(2)}, u32[]{:S(2)}) collective-permute-start(bf16[128,128]{1,0:T(8,128)(2,1)S(1)} %pad_maximum_fusion.8), channel_id=1, source_target_pairs={{0,16},{4,20},{8,24},{12,28},{16,32},{20,36},{24,40},{28,44},{32,4... | collective-permute-start | bytes 98312 | tf_op jit(solution)/shard_map/ppermute | solution.py:16
  35.6 104.5 %collective-permute-start = (s32[1]{0:T(128)}, s32[1]{0:T(128)}, u32[]{:S(2)}, u32[]{:S(2)}) collective-permute-start(s32[1]{0:T(128)} %param.30), channel_id=1, source_target_pairs={{0,28},{4,32},{8,36},{12,40},{16,44},{20,48},{24,52},{28,56},{32,6... | collective-permute-start | bytes 20 | tf_op jit(solution)/shard_map/ppermute | solution.py:16
  42.0 218.1 %all-to-all-start = ((bf16[128,2,128]{2,1,0:T(2,128)(2,1)}), bf16[128,2,128]{2,1,0:T(2,128)(2,1)S(1)}, u32[]{:S(2)}, u32[]{:S(2)}) async-start(bf16[128,2,128]{2,1,0:T(2,128)(2,1)} %stack.105), calls=%async_computation | async-start | bytes 131072 | tf_op jit(solution)/shard_map/all_to_all | solution.py:101
  53.6 778.5 %all-reduce.8.cloned.1.call-start = ((), (), s32[]{:S(2)}) async-start(), calls=%async_computation.1 | async-start | bytes 262144
  134.3 1.5 copy-start.3
  134.3 1.5 copy-start.10
  137.6 71.4 %copy-start.7 = (bf16[128,1,128]{2,0,1:T(8,128)(2,1)S(1)}, bf16[128,1,128]{2,0,1:T(8,128)(2,1)}, u32[]{:S(2)}) copy-start(bf16[128,1,128]{2,0,1:T(8,128)(2,1)} %param.21) | copy-start | bytes 98308
  137.7 97.5 %copy-start.5 = (s32[130]{0:T(256)S(1)}, s32[130]{0:T(256)}, u32[]{:S(2)}) copy-start(s32[130]{0:T(256)} %constant.212.clone.2) | copy-start | bytes 1564
  137.7 97.5 %copy-start.6 = (s32[130]{0:T(256)S(1)}, s32[130]{0:T(256)}, u32[]{:S(2)}) copy-start(s32[130]{0:T(256)} %constant.214.clone.2) | copy-start | bytes 1564
  140.1 3.7 collective-permute-start.1
  143.8 8.1 collective-permute-start.2
  151.9 5.9 collective-permute-start.3
  157.8 9.5 %collective-permute-start.4 = (s32[1]{0:T(128)}, s32[1]{0:T(128)}, u32[]{:S(2)}, u32[]{:S(2)}) collective-permute-start(s32[1]{0:T(128)} %param.30), channel_id=1, source_target_pairs={{0,12},{4,16},{8,20},{12,24},{16,28},{20,32},{24,36},{28,40},{32,4... | collective-permute-start | bytes 20 | tf_op jit(solution)/shard_map/ppermute | solution.py:16
  167.3 2.5 collective-permute-start.5
  169.8 7.3 collective-permute-start.6
  177.1 40.7 %collective-permute-start.11 = (bf16[128,128]{1,0:T(8,128)(2,1)S(1)}, bf16[128,128]{1,0:T(8,128)(2,1)S(1)}, u32[]{:S(2)}, u32[]{:S(2)}) collective-permute-start(bf16[128,128]{1,0:T(8,128)(2,1)S(1)} %pad_maximum_fusion.8), channel_id=1, source_target_pairs={{0,12},{4,16},{8,20},{12,24},{16,28},{20,32},{24,36},{28,40},{32,4... | collective-permute-start | bytes 98312 | tf_op jit(solution)/shard_map/ppermute | solution.py:16
  199.5 22.0 %collective-permute-start.12 = (bf16[128,128]{1,0:T(8,128)(2,1)S(1)}, bf16[128,128]{1,0:T(8,128)(2,1)S(1)}, u32[]{:S(2)}, u32[]{:S(2)}) collective-permute-start(bf16[128,128]{1,0:T(8,128)(2,1)S(1)} %pad_maximum_fusion.8), channel_id=1, source_target_pairs={{0,8},{4,12},{8,16},{12,20},{16,24},{20,28},{24,32},{28,36},{32,40... | collective-permute-start | bytes 98312 | tf_op jit(solution)/shard_map/ppermute | solution.py:16
  205.2 20.3 %collective-permute-start.13 = (bf16[128,128]{1,0:T(8,128)(2,1)S(1)}, bf16[128,128]{1,0:T(8,128)(2,1)S(1)}, u32[]{:S(2)}, u32[]{:S(2)}) collective-permute-start(bf16[128,128]{1,0:T(8,128)(2,1)S(1)} %pad_maximum_fusion.8), channel_id=1, source_target_pairs={{0,4},{4,8},{8,12},{12,16},{16,20},{20,24},{24,28},{28,32},{32,36}... | collective-permute-start | bytes 98312 | tf_op jit(solution)/shard_map/ppermute | solution.py:16
  208.9 45.2 %collective-permute-start.14 = (bf16[128,128]{1,0:T(8,128)(2,1)S(1)}, bf16[128,128]{1,0:T(8,128)(2,1)S(1)}, u32[]{:S(2)}, u32[]{:S(2)}) collective-permute-start(bf16[128,128]{1,0:T(8,128)(2,1)S(1)} %bitcast.350), channel_id=1, source_target_pairs={{0,28},{4,32},{8,36},{12,40},{16,44},{20,48},{24,52},{28,56},{32,6... | collective-permute-start | bytes 98312 | tf_op jit(solution)/shard_map/ppermute | solution.py:16
  212.9 43.1 %collective-permute-start.15 = (bf16[128,128]{1,0:T(8,128)(2,1)S(1)}, bf16[128,128]{1,0:T(8,128)(2,1)S(1)}, u32[]{:S(2)}, u32[]{:S(2)}) collective-permute-start(bf16[128,128]{1,0:T(8,128)(2,1)S(1)} %bitcast.351), channel_id=1, source_target_pairs={{0,24},{4,28},{8,32},{12,36},{16,40},{20,44},{24,48},{28,52},{32,5... | collective-permute-start | bytes 98312 | tf_op jit(solution)/shard_map/ppermute | solution.py:16
  217.8 41.2 %collective-permute-start.16 = (bf16[128,128]{1,0:T(8,128)(2,1)S(1)}, bf16[128,128]{1,0:T(8,128)(2,1)S(1)}, u32[]{:S(2)}, u32[]{:S(2)}) collective-permute-start(bf16[128,128]{1,0:T(8,128)(2,1)S(1)} %bitcast.352), channel_id=1, source_target_pairs={{0,20},{4,24},{8,28},{12,32},{16,36},{20,40},{24,44},{28,48},{32,5... | collective-permute-start | bytes 98312 | tf_op jit(solution)/shard_map/ppermute | solution.py:16
  221.5 37.5 %collective-permute-start.17 = (bf16[128,128]{1,0:T(8,128)(2,1)S(1)}, bf16[128,128]{1,0:T(8,128)(2,1)S(1)}, u32[]{:S(2)}, u32[]{:S(2)}) collective-permute-start(bf16[128,128]{1,0:T(8,128)(2,1)S(1)} %bitcast.353), channel_id=1, source_target_pairs={{0,16},{4,20},{8,24},{12,28},{16,32},{20,36},{24,40},{28,44},{32,4... | collective-permute-start | bytes 98312 | tf_op jit(solution)/shard_map/ppermute | solution.py:16
  225.5 33.6 %collective-permute-start.18 = (bf16[128,128]{1,0:T(8,128)(2,1)S(1)}, bf16[128,128]{1,0:T(8,128)(2,1)S(1)}, u32[]{:S(2)}, u32[]{:S(2)}) collective-permute-start(bf16[128,128]{1,0:T(8,128)(2,1)S(1)} %bitcast.354), channel_id=1, source_target_pairs={{0,12},{4,16},{8,20},{12,24},{16,28},{20,32},{24,36},{28,40},{32,4... | collective-permute-start | bytes 98312 | tf_op jit(solution)/shard_map/ppermute | solution.py:16
  254.1 4.9 collective-permute-start.19
  256.1 3.9 collective-permute-start.20
  301.2 495.3 %collective-permute-start.21 = (bf16[128,128]{1,0:T(8,128)(2,1)S(1)}, bf16[128,128]{1,0:T(8,128)(2,1)S(1)}, u32[]{:S(2)}, u32[]{:S(2)}) collective-permute-start(bf16[128,128]{1,0:T(8,128)(2,1)S(1)} %get-tuple-element.575), channel_id=1, source_target_pairs={{4,0},{8,4},{12,8},{16,12},{20,16},{24,20},{28,24},{32,28},{36,32}... | collective-permute-start | bytes 98312 | tf_op jit(solution)/shard_map/ppermute | solution.py:16
  303.1 494.7 %collective-permute-start.22 = (bf16[128,128]{1,0:T(8,128)(2,1)S(1)}, bf16[128,128]{1,0:T(8,128)(2,1)S(1)}, u32[]{:S(2)}, u32[]{:S(2)}) collective-permute-start(bf16[128,128]{1,0:T(8,128)(2,1)S(1)} %get-tuple-element.581), channel_id=1, source_target_pairs={{8,0},{12,4},{16,8},{20,12},{24,16},{28,20},{32,24},{36,28},{40,32... | collective-permute-start | bytes 98312 | tf_op jit(solution)/shard_map/ppermute | solution.py:16
  304.4 496.6 %collective-permute-start.23 = (bf16[128,128]{1,0:T(8,128)(2,1)S(1)}, bf16[128,128]{1,0:T(8,128)(2,1)S(1)}, u32[]{:S(2)}, u32[]{:S(2)}) collective-permute-start(bf16[128,128]{1,0:T(8,128)(2,1)S(1)} %get-tuple-element.580), channel_id=1, source_target_pairs={{12,0},{16,4},{20,8},{24,12},{28,16},{32,20},{36,24},{40,28},{44,3... | collective-permute-start | bytes 98312 | tf_op jit(solution)/shard_map/ppermute | solution.py:16
  305.7 502.9 %collective-permute-start.24 = (bf16[128,128]{1,0:T(8,128)(2,1)S(1)}, bf16[128,128]{1,0:T(8,128)(2,1)S(1)}, u32[]{:S(2)}, u32[]{:S(2)}) collective-permute-start(bf16[128,128]{1,0:T(8,128)(2,1)S(1)} %get-tuple-element.579), channel_id=1, source_target_pairs={{16,0},{20,4},{24,8},{28,12},{32,16},{36,20},{40,24},{44,28},{48,3... | collective-permute-start | bytes 98312 | tf_op jit(solution)/shard_map/ppermute | solution.py:16
  307.0 502.9 %collective-permute-start.25 = (bf16[128,128]{1,0:T(8,128)(2,1)S(1)}, bf16[128,128]{1,0:T(8,128)(2,1)S(1)}, u32[]{:S(2)}, u32[]{:S(2)}) collective-permute-start(bf16[128,128]{1,0:T(8,128)(2,1)S(1)} %get-tuple-element.578), channel_id=1, source_target_pairs={{20,0},{24,4},{28,8},{32,12},{36,16},{40,20},{44,24},{48,28},{52,3... | collective-permute-start | bytes 98312 | tf_op jit(solution)/shard_map/ppermute | solution.py:16
  308.5 0.9 copy-start.1
  310.7 503.5 %copy-start = (bf16[128,1,128]{2,0,1:T(8,128)(2,1)S(1)}, bf16[128,1,128]{2,0,1:T(8,128)(2,1)}, u32[]{:S(2)}) copy-start(bf16[128,1,128]{2,0,1:T(8,128)(2,1)} %param.20) | copy-start | bytes 98308
  796.4 14.8 %collective-permute-start.26 = (bf16[128,128]{1,0:T(8,128)(2,1)S(1)}, bf16[128,128]{1,0:T(8,128)(2,1)S(1)}, u32[]{:S(2)}, u32[]{:S(2)}) collective-permute-start(bf16[128,128]{1,0:T(8,128)(2,1)S(1)} %get-tuple-element.577), channel_id=1, source_target_pairs={{24,0},{28,4},{32,8},{36,12},{40,16},{44,20},{48,24},{52,28},{56,3... | collective-permute-start | bytes 98312 | tf_op jit(solution)/shard_map/ppermute | solution.py:16
  797.7 14.8 %collective-permute-start.27 = (bf16[128,128]{1,0:T(8,128)(2,1)S(1)}, bf16[128,128]{1,0:T(8,128)(2,1)S(1)}, u32[]{:S(2)}, u32[]{:S(2)}) collective-permute-start(bf16[128,128]{1,0:T(8,128)(2,1)S(1)} %get-tuple-element.576), channel_id=1, source_target_pairs={{28,0},{32,4},{36,8},{40,12},{44,16},{48,20},{52,24},{56,28},{60,3... | collective-permute-start | bytes 98312 | tf_op jit(solution)/shard_map/ppermute | solution.py:16
  799.6 33.3 %copy-start.8 = (bf16[2,1,128]{2,0,1:T(2,128)(2,1)S(1)}, bf16[2,1,128]{2,0,1:T(2,128)(2,1)}, u32[]{:S(2)}) copy-start(bf16[2,1,128]{2,0,1:T(2,128)(2,1)} %param.25) | copy-start | bytes 1540
  801.0 13.4 %collective-permute-start.28 = (bf16[128,128]{1,0:T(8,128)(2,1)S(1)}, bf16[128,128]{1,0:T(8,128)(2,1)S(1)}, u32[]{:S(2)}, u32[]{:S(2)}) collective-permute-start(bf16[128,128]{1,0:T(8,128)(2,1)S(1)} %get-tuple-element.568), channel_id=1, source_target_pairs={{4,0},{8,4},{12,8},{16,12},{20,16},{24,20},{28,24},{32,28},{36,32}... | collective-permute-start | bytes 98312 | tf_op jit(solution)/shard_map/ppermute | solution.py:16
  808.6 7.1 collective-permute-start.29
  809.9 7.1 collective-permute-start.30
  811.2 7.5 collective-permute-start.31
  812.5 10.3 %collective-permute-start.32 = (bf16[128,128]{1,0:T(8,128)(2,1)S(1)}, bf16[128,128]{1,0:T(8,128)(2,1)S(1)}, u32[]{:S(2)}, u32[]{:S(2)}) collective-permute-start(bf16[128,128]{1,0:T(8,128)(2,1)S(1)} %get-tuple-element.571), channel_id=1, source_target_pairs={{20,0},{24,4},{28,8},{32,12},{36,16},{40,20},{44,24},{48,28},{52,3... | collective-permute-start | bytes 98312 | tf_op jit(solution)/shard_map/ppermute | solution.py:16
  814.4 11.1 %collective-permute-start.33 = (bf16[128,128]{1,0:T(8,128)(2,1)S(1)}, bf16[128,128]{1,0:T(8,128)(2,1)S(1)}, u32[]{:S(2)}, u32[]{:S(2)}) collective-permute-start(bf16[128,128]{1,0:T(8,128)(2,1)S(1)} %get-tuple-element.570), channel_id=1, source_target_pairs={{24,0},{28,4},{32,8},{36,12},{40,16},{44,20},{48,24},{52,28},{56,3... | collective-permute-start | bytes 98312 | tf_op jit(solution)/shard_map/ppermute | solution.py:16
  815.7 15.0 %collective-permute-start.34 = (bf16[128,128]{1,0:T(8,128)(2,1)S(1)}, bf16[128,128]{1,0:T(8,128)(2,1)S(1)}, u32[]{:S(2)}, u32[]{:S(2)}) collective-permute-start(bf16[128,128]{1,0:T(8,128)(2,1)S(1)} %get-tuple-element.569), channel_id=1, source_target_pairs={{28,0},{32,4},{36,8},{40,12},{44,16},{48,20},{52,24},{56,28},{60,3... | collective-permute-start | bytes 98312 | tf_op jit(solution)/shard_map/ppermute | solution.py:16
  (1 other events, 0.9 us)
Sparse Core Ops, SparseCore 0:
  301.2 316.7 all-reduce.7
